TPU v7x, 32 devices: a whole 2x2x4 slice. The times are simulated.
32 devices in a mesh: win: 4 (over y, x), seq: 8 (over z, core).
Axes of the slice: x: 2, y: 2, z: 4, core: 2. Of those that a mesh axis runs over, the one named last changes fastest.
Arguments:
- conv_input: bfloat16 [384, 8192], P(None, ('win', 'seq')), parts along dimension 1, may hold values from -36 to 36, as said below
- near_weight: bfloat16 [5, 384, 384], P(None, 'seq'), may hold values from -0.125 to 0.125
- near_bias: float32 [384], replicated, may hold values from -3 to 3
- near_gain: float32 [384], replicated, may hold values from 0.25 to 1.75
- dilated_weight: bfloat16 [5, 384, 384], P(None, 'seq'), may hold values from -0.125 to 0.125
- dilated_bias: float32 [384], replicated, may hold values from -3 to 3
- far_gain: float32 [384], replicated, may hold values from 0.25 to 1.75
- pool_weight: bfloat16 [2, 384, 1536], P(None, None, 'seq'), may hold values from -0.21875 to 0.21875
- attn_gain: float32 [1536], replicated, may hold values from 0.25 to 1.75
- query_weight: bfloat16 [1536, 256], replicated, may hold values from -32 to 32
- key_weight: bfloat16 [1536, 256], replicated, may hold values from -1 to 1
- value_weight: bfloat16 [1536, 768], P('seq'), may hold values from -0.15625 to 0.15625
Outputs:
- attended: bfloat16 [4096, 768], P(('win', 'seq')), parts along dimension 0
There are 4 independent parts, one for each index of `win`. A program takes and returns all parts, laid end to end along the dimension named above; an argument that names none is the same for every part. Nothing has to cross between parts.
Inputs may be any that keep to these rules, and one draw needn't show every extreme that they name: `conv_input`: features of the window; channels and positions have their own scales.
All inputs are finite; a program needn't handle non-finite values.
Results may differ from a plain program's by a relative error of at most 0.02.
Values may be sent and summed in bfloat16 or wider, within the bound.
A program may use at most 64 MiB of HBM per device.

v0:
```python
import jax
import jax.numpy as jnp
from jax import lax
from jax.sharding import PartitionSpec as P

HEADS = 4
KEY = 64
VAL = 192
KS = 5
DILATION_STEP = 16


def padded_2(block, sides, width):
    for axis, dim in sides:
        count = lax.axis_size(axis)
        forward = [(i, i + 1) for i in range(count - 1)]
        backward = [(target, source) for source, target in forward]
        low = lax.ppermute(
            lax.slice_in_dim(block, block.shape[dim] - width, None, axis=dim), axis, forward
        )
        high = lax.ppermute(lax.slice_in_dim(block, 0, width, axis=dim), axis, backward)
        block = jnp.concatenate([low, block, high], axis=dim)
    return block


def activate(field, gain):
    wide = field.astype(jnp.float32)
    square = jnp.mean(wide * wide, axis=0, keepdims=True)
    scaled = wide * lax.rsqrt(square + 1e-06) * gain[:, None]
    return jax.nn.gelu(scaled, approximate=False).astype(jnp.bfloat16)


def convolution_taps(padded, weight, spread):
    length = padded.shape[1] - 4 * spread
    stacked = jnp.stack([padded[:, t * spread : t * spread + length] for t in range(KS)])
    return jnp.einsum("toc,tcl->ol", weight, stacked, preferred_element_type=jnp.float32)


def attend_step(carry, pieces, queries, heads):
    running_top, running_sum, running_acc = carry
    keys, values = pieces
    count = keys.shape[0]
    key_heads = keys.reshape(count, heads, -1)
    value_heads = values.reshape(count, heads, -1)
    value_size = value_heads.shape[2]
    scores = jnp.einsum("phk,nhk->hpn", queries, key_heads, preferred_element_type=jnp.float32)
    new_top = jnp.maximum(running_top, jnp.max(scores, axis=-1))
    factor = jnp.exp(running_top - new_top)
    raised = jnp.exp(scores - new_top[:, :, None])
    new_sum = jnp.sum(raised, axis=-1)
    summed = jnp.einsum(
        "hpn,nhv->phv", raised.astype(jnp.bfloat16), value_heads, preferred_element_type=jnp.float32
    )
    widened = jnp.repeat(jnp.transpose(factor), value_size, axis=1)
    new_acc = running_acc * widened + summed.reshape(summed.shape[0], heads * value_size)
    return (new_top, new_sum, new_acc)


def shards(
    conv_input,
    near_weight,
    near_bias,
    near_gain,
    dilated_weight,
    dilated_bias,
    far_gain,
    pool_weight,
    attn_gain,
    query_weight,
    key_weight,
    value_weight,
):
    near_taps, dilated_taps, pool_taps = (
        lax.all_gather(near_weight, "seq", axis=1, tiled=True),
        lax.all_gather(dilated_weight, "seq", axis=1, tiled=True),
        lax.all_gather(pool_weight, "seq", axis=2, tiled=True),
    )
    near_act = activate(conv_input, near_gain)
    near_pad = padded_2(near_act, (("seq", 1),), 2)
    local_output = (
        conv_input.astype(jnp.float32)
        + near_bias[:, None]
        + convolution_taps(near_pad, near_taps, 1)
    ).astype(jnp.bfloat16)
    dilated_activation = activate(local_output, far_gain)
    dilated_padding = padded_2(dilated_activation, (("seq", 1),), 2 * DILATION_STEP)
    dilated_output = (
        local_output.astype(jnp.float32)
        + dilated_bias[:, None]
        + convolution_taps(dilated_padding, dilated_taps, DILATION_STEP)
    ).astype(jnp.bfloat16)
    pool_act = jax.nn.gelu(dilated_output.astype(jnp.float32), approximate=False).astype(
        jnp.bfloat16
    )
    pooled = jnp.einsum(
        "cp,cd->pd", pool_act[:, 0::2], pool_taps[0], preferred_element_type=jnp.float32
    )
    pooled = pooled + jnp.einsum(
        "cp,cd->pd", pool_act[:, 1::2], pool_taps[1], preferred_element_type=jnp.float32
    )
    square = jnp.mean(pooled * pooled, axis=1, keepdims=True)
    normed = (pooled * lax.rsqrt(square + 1e-06) * attn_gain[None, :]).astype(jnp.bfloat16)
    queries = (
        jnp.dot(normed, query_weight, preferred_element_type=jnp.float32) * KEY ** (-0.5)
    ).astype(jnp.bfloat16)
    keys = jnp.dot(normed, key_weight, preferred_element_type=jnp.float32).astype(jnp.bfloat16)
    rows = normed.shape[0]
    values = jnp.dot(
        normed,
        lax.all_gather(value_weight, "seq", axis=0, tiled=True),
        preferred_element_type=jnp.float32,
    ).astype(jnp.bfloat16)
    query_heads = queries.reshape(rows, HEADS, KEY)
    start_carry = (
        jnp.full((HEADS, rows), -1e30, jnp.float32),
        jnp.zeros((HEADS, rows), jnp.float32),
        jnp.zeros((rows, HEADS * VAL), jnp.float32),
    )
    final = attend_step(
        start_carry,
        (
            lax.all_gather(keys, "seq", axis=0, tiled=True),
            lax.all_gather(values, "seq", axis=0, tiled=True),
        ),
        query_heads,
        HEADS,
    )
    final_top, final_sum, final_acc = final
    denom = jnp.repeat(jnp.transpose(final_sum), VAL, axis=1)
    return (final_acc / denom).astype(jnp.bfloat16)


def solution(mesh):
    placed = (
        P(None, ("win", "seq")),
        P(None, "seq", None),
        P(),
        P(),
        P(None, "seq", None),
        P(),
        P(),
        P(None, None, "seq"),
        P(),
        P(),
        P(),
        P("seq", None),
    )
    return jax.shard_map(
        shards, mesh=mesh, in_specs=placed, out_specs=P(("win", "seq"), None), check_vma=False
    )
```

profile of v0, /device:TPU:1, one launch (start us, length us, event | category | flops | bytes accessed | tf_op | source)
XLA Modules:
  0.0 166.6 jit_solution(11077458214553701075)
XLA Ops:
  6.5 0.0 copy-start
  6.5 0.0 copy-start.3
  6.5 0.0 all-gather.6.cloned.1.call-start
  6.5 0.7 all-gather.6.cloned.1.call-update
  7.3 0.0 all-gather.8.cloned.1.call-start
  7.3 0.7 all-gather.8.cloned.1.call-update
  8.0 0.0 all-gather.10.cloned.1.call-start
  8.1 0.7 all-gather.10.cloned.1.call-update
  8.7 0.0 all-gather.12.cloned.1.call-start
  8.8 1.1 copy.18
  9.9 0.1 fusion.15
  10.0 1.7 fusion.20
  11.7 4.6 %collective-permute-start = (bf16[384,2]{0,1:T(2,128)(2,1)S(1)}, bf16[384,2]{0,1:T(2,128)(2,1)S(1)}, u32[]{:S(2)}, u32[]{:S(2)}) collective-permute-start(bf16[384,2]{0,1:T(2,128)(2,1)S(1)} %get-tuple-element.8), channel_id=1, source_target_pairs={{0,1},{1,2},{2,3},{3,4},{4,5},{5,6},{6,7},{8,9},{9,10},{10,11},{11... | collective-permute-start | bytes 4616 | tf_op jit(solution)/shard_map/ppermute | solution.py:18
  16.3 1.9 %collective-permute-start.1 = (bf16[384,2]{0,1:T(2,128)(2,1)S(1)}, bf16[384,2]{0,1:T(2,128)(2,1)S(1)}, u32[]{:S(2)}, u32[]{:S(2)}) collective-permute-start(bf16[384,2]{0,1:T(2,128)(2,1)S(1)} %get-tuple-element.7), channel_id=1, source_target_pairs={{1,0},{2,1},{3,2},{4,3},{5,4},{6,5},{7,6},{9,8},{10,9},{11,10},{12... | collective-permute-start | bytes 4616 | tf_op jit(solution)/shard_map/ppermute | solution.py:21
  18.2 0.0 all-gather.12.cloned.1.call-update
  18.2 0.0 all-gather.14.cloned.1.call-start
  18.3 0.0 collective-permute-done
  18.3 0.1 fusion.64
  18.4 0.1 fusion.78
  18.4 0.0 copy-done.3
  18.4 0.0 copy-start.4
  18.5 1.0 bitcast_dynamic-update-slice_fusion.1
  19.5 1.7 %collective-permute-done.1 = bf16[384,2]{0,1:T(2,128)(2,1)S(1)} collective-permute-done((bf16[384,2]{0,1:T(2,128)(2,1)S(1)}, bf16[384,2]{0,1:T(2,128)(2,1)S(1)}, u32[]{:S(2)}, u32[]{:S(2)}) %collective-permute-start.1) | collective-permute-done | bytes 1568 | tf_op jit(solution)/shard_map/ppermute | solution.py:21
  21.2 0.1 fusion.61
  21.3 0.1 fusion.76
  21.3 14.7 %all-gather.6.cloned.1.call-done = bf16[5,384,384]{2,1,0:T(8,128)(2,1)} async-done(((bf16[5,48,384]{2,1,0:T(8,128)(2,1)}), bf16[5,384,384]{2,1,0:T(8,128)(2,1)}) %all-gather.6.cloned.1.call-update) | async-done | bytes 1474576 | tf_op jit(solution)/shard_map/all_gather | solution.py:74
  36.0 0.0 copy-done.5
  36.0 2.2 %multiply_reduce_fusion.1 = (f32[256]{0:T(256)S(1)}, f32[384,256]{0,1:T(8,128)S(1)}) fusion(bf16[5,384,256]{1,2,0:T(8,128)(2,1)S(1)} %fusion.76, bf16[5,384,384]{2,1,0:T(8,128)(2,1)} %all-gather.6.cloned.1.call-done, f32[384]{0:T(512)S(1)} %copy-done.5, bf16[384,256]{0,1:T(8,128)(2,1)S(1)} %copy.18), kind=kOutput, calls=%fused_computation.78 | convolution fusion | flops 378175232 | bytes 3049984 | tf_op jit(solution)/shard_map/toc,tcl->ol/dot_general | solution.py:36
  38.2 0.0 copy-start.6
  38.2 0.0 copy-done.4
  38.2 1.0 fusion.30
  39.2 2.9 %collective-permute-start.2 = (bf16[384,32]{0,1:T(8,128)(2,1)S(1)}, bf16[384,32]{0,1:T(8,128)(2,1)S(1)}, u32[]{:S(2)}, u32[]{:S(2)}) collective-permute-start(bf16[384,32]{0,1:T(8,128)(2,1)S(1)} %get-tuple-element.6), channel_id=1, source_target_pairs={{0,1},{1,2},{2,3},{3,4},{4,5},{5,6},{6,7},{8,9},{9,10},{10,11},{11... | collective-permute-start | bytes 73736 | tf_op jit(solution)/shard_map/ppermute | solution.py:18
  42.1 1.9 %collective-permute-start.3 = (bf16[384,32]{0,1:T(8,128)(2,1)S(1)}, bf16[384,32]{0,1:T(8,128)(2,1)S(1)}, u32[]{:S(2)}, u32[]{:S(2)}) collective-permute-start(bf16[384,32]{0,1:T(8,128)(2,1)S(1)} %get-tuple-element.5), channel_id=1, source_target_pairs={{1,0},{2,1},{3,2},{4,3},{5,4},{6,5},{7,6},{9,8},{10,9},{11,10},{12... | collective-permute-start | bytes 73736 | tf_op jit(solution)/shard_map/ppermute | solution.py:21
  44.0 0.0 collective-permute-done.2
  44.1 1.0 bitcast_dynamic-update-slice_fusion
  45.1 2.9 %collective-permute-done.3 = bf16[384,32]{0,1:T(8,128)(2,1)S(1)} collective-permute-done((bf16[384,32]{0,1:T(8,128)(2,1)S(1)}, bf16[384,32]{0,1:T(8,128)(2,1)S(1)}, u32[]{:S(2)}, u32[]{:S(2)}) %collective-permute-start.3) | collective-permute-done | bytes 24608 | tf_op jit(solution)/shard_map/ppermute | solution.py:21
  48.1 13.4 %all-gather.8.cloned.1.call-done = bf16[5,384,384]{2,1,0:T(8,128)(2,1)} async-done(((bf16[5,48,384]{2,1,0:T(8,128)(2,1)}), bf16[5,384,384]{2,1,0:T(8,128)(2,1)}) %all-gather.8.cloned.1.call-update) | async-done | bytes 1474576 | tf_op jit(solution)/shard_map/all_gather | solution.py:75
  61.5 0.0 copy-done.6
  61.5 2.9 %fusion.33 = bf16[384,256]{0,1:T(8,128)(2,1)S(1)} fusion(bf16[5,384,256]{1,2,0:T(8,128)(2,1)S(1)} %fusion.72, bf16[5,384,384]{2,1,0:T(8,128)(2,1)} %all-gather.8.cloned.1.call-done, f32[384,256]{0,1:T(8,128)S(1)} %get-tuple-element.12, f32[384]{0:T(512)S(1)} %copy-done.6), kind=kOutput, calls=%fused_computation.50 | convolution fusion | flops 384270336 | bytes 3048960 | tf_op jit(solution)/shard_map/toc,tcl->ol/dot_general | solution.py:36
  64.4 0.2 slice.68
  64.6 0.2 slice.70
  64.8 0.0 copy-start.2
  64.8 29.1 %all-gather.10.cloned.1.call-done = bf16[2,384,1536]{1,2,0:T(8,128)(2,1)} async-done(((bf16[2,384,192]{1,2,0:T(8,128)(2,1)}), bf16[2,384,1536]{1,2,0:T(8,128)(2,1)}) %all-gather.10.cloned.1.call-update) | async-done | bytes 2359312 | tf_op jit(solution)/shard_map/all_gather | solution.py:76
  93.9 1.8 %fusion.6 = f32[128,1536]{1,0:T(8,128)S(1)} fusion(bf16[384,128]{0,1:T(8,128)(2,1)S(1)} %slice.68, bf16[2,384,1536]{1,2,0:T(8,128)(2,1)} %all-gather.10.cloned.1.call-done), kind=kOutput, calls=%fused_computation.13 | convolution fusion | flops 150994944 | bytes 2064384 | tf_op jit(solution)/shard_map/cp,cd->pd/dot_general | solution.py:95
  95.7 1.9 %multiply_reduce_fusion = (f32[128]{0:T(128)S(1)}, f32[128,1536]{1,0:T(8,128)S(1)}) fusion(f32[128,1536]{1,0:T(8,128)S(1)} %fusion.6, bf16[384,128]{0,1:T(8,128)(2,1)S(1)} %slice.70, bf16[2,384,1536]{1,2,0:T(8,128)(2,1)} %all-gather.10.cloned.1.call-done), kind=kOutput, calls=%fused_computation.25 | convolution fusion | flops 151584640 | bytes 2851328 | tf_op jit(solution)/shard_map/cp,cd->pd/dot_general | solution.py:98
  97.6 0.0 copy-done.2
  97.6 0.1 multiply_convert_fusion
  97.7 0.0 copy-start.1
  97.7 28.4 %all-gather.12.cloned.1.call-done = bf16[1536,768]{1,0:T(8,128)(2,1)} async-done(((bf16[192,768]{1,0:T(8,128)(2,1)}), bf16[1536,768]{1,0:T(8,128)(2,1)}) %all-gather.12.cloned.1.call-update) | async-done | bytes 2359312 | tf_op jit(solution)/shard_map/all_gather | solution.py:110
  126.1 2.8 %convolution_convert_fusion = bf16[128,768]{1,0:T(8,128)(2,1)} fusion(bf16[128,1536]{1,0:T(8,128)(2,1)S(1)} %multiply_convert_fusion, bf16[1536,768]{1,0:T(8,128)(2,1)} %all-gather.12.cloned.1.call-done), kind=kOutput, calls=%fused_computation.15 | convolution fusion | flops 302088192 | bytes 2949120 | tf_op jit(solution)/shard_map/dot_general | solution.py:108
  129.0 0.0 all-gather.14.cloned.1.call-update
  129.0 0.0 copy-done
  129.0 0.3 fusion.12
  129.3 0.1 copy.19
  129.4 0.0 copy-done.1
  129.4 0.3 convolution_convert_fusion.1
  129.7 16.5 %all_gather.21 = bf16[1024,256]{1,0:T(8,128)(2,1)S(1)} all-gather(bf16[128,256]{1,0:T(8,128)(2,1)S(1)} %convolution_convert_fusion.1), channel_id=1, replica_groups=mesh['win'=4,'seq'=8] {'seq'}, dimensions={0}, use_global_device_ids=true | all-gather | bytes 589824 | tf_op jit(solution)/shard_map/all_gather | solution.py:122
  146.2 0.2 copy.20
  146.4 0.6 fusion.81
  147.0 0.5 fusion
  147.5 7.1 %all-gather.14.cloned.1.call-done = bf16[1024,768]{1,0:T(8,128)(2,1)} async-done(((bf16[128,768]{1,0:T(8,128)(2,1)}), bf16[1024,768]{1,0:T(8,128)(2,1)}) %all-gather.14.cloned.1.call-update) | async-done | bytes 1572880 | tf_op jit(solution)/shard_map/all_gather | solution.py:123
  154.6 2.6 %copy.21 = bf16[1024,768]{0,1:T(8,128)(2,1)} copy(bf16[1024,768]{1,0:T(8,128)(2,1)} %all-gather.14.cloned.1.call-done) | data formatting | bytes 3145728 | tf_op jit(solution)/shard_map/all_gather | solution.py:123
  157.2 2.1 %fusion.7 = bf16[128,4,192]{0,2,1:T(8,128)(2,1)S(1)} fusion(bf16[1024,4,192]{0,2,1:T(8,128)(2,1)} %bitcast.97, f32[4,128,1024]{2,1,0:T(8,128)S(1)} %get-tuple-element.16, f32[4,128]{1,0:T(4,128)S(1)} %get-tuple-element.10, f32[128,4]{0,1:T(4,128)S(1)} %bitcast.100, f32[128,4]{0,1:T(4,128)S(1)} %get-tuple-element.9), kind=kOutput, calls=%fused_computation.14 | convolution fusion | flops 202670080 | bytes 3872768 | tf_op jit(solution)/shard_map/hpn,nhv->phv/dot_general | solution.py:51
  159.3 0.8 copy.22
  (11 shorter events, 0.2 us)
Async XLA Ops:
  6.5 122.5 %copy-start = (bf16[1536,256]{1,0:T(8,128)(2,1)S(1)}, bf16[1536,256]{1,0:T(8,128)(2,1)}, u32[]{:S(2)}) copy-start(bf16[1536,256]{1,0:T(8,128)(2,1)} %param.21) | copy-start | bytes 2359300
  6.5 11.9 %copy-start.3 = (f32[384]{0:T(512)S(1)}, f32[384]{0:T(512)}, u32[]{:S(2)}) copy-start(f32[384]{0:T(512)} %param.15) | copy-start | bytes 4612
  6.5 29.5 %copy-start.5 = (f32[384]{0:T(512)S(1)}, f32[384]{0:T(512)}, u32[]{:S(2)}) copy-start(f32[384]{0:T(512)} %param.14) | copy-start | bytes 4612
  6.5 29.5 %all-gather.6.cloned.1.call-start = ((), (), s32[]{:S(2)}) async-start(), calls=%async_computation | async-start | bytes 1658880 | tf_op jit(solution)/shard_map/all_gather | solution.py:74
  7.3 54.2 %all-gather.8.cloned.1.call-start = ((), (), s32[]{:S(2)}) async-start(), calls=%async_computation.1 | async-start | bytes 1658880 | tf_op jit(solution)/shard_map/all_gather | solution.py:75
  8.0 85.9 %all-gather.10.cloned.1.call-start = ((), (), s32[]{:S(2)}) async-start(), calls=%async_computation.2 | async-start | bytes 2654208 | tf_op jit(solution)/shard_map/all_gather | solution.py:76
  8.7 117.4 %all-gather.12.cloned.1.call-start = ((), (), s32[]{:S(2)}) async-start(), calls=%async_computation.3 | async-start | bytes 2654208 | tf_op jit(solution)/shard_map/all_gather | solution.py:110
  11.7 6.6 %collective-permute-start = (bf16[384,2]{0,1:T(2,128)(2,1)S(1)}, bf16[384,2]{0,1:T(2,128)(2,1)S(1)}, u32[]{:S(2)}, u32[]{:S(2)}) collective-permute-start(bf16[384,2]{0,1:T(2,128)(2,1)S(1)} %get-tuple-element.8), channel_id=1, source_target_pairs={{0,1},{1,2},{2,3},{3,4},{4,5},{5,6},{6,7},{8,9},{9,10},{10,11},{11... | collective-permute-start | bytes 4616 | tf_op jit(solution)/shard_map/ppermute | solution.py:18
  16.3 4.9 %collective-permute-start.1 = (bf16[384,2]{0,1:T(2,128)(2,1)S(1)}, bf16[384,2]{0,1:T(2,128)(2,1)S(1)}, u32[]{:S(2)}, u32[]{:S(2)}) collective-permute-start(bf16[384,2]{0,1:T(2,128)(2,1)S(1)} %get-tuple-element.7), channel_id=1, source_target_pairs={{1,0},{2,1},{3,2},{4,3},{5,4},{6,5},{7,6},{9,8},{10,9},{11,10},{12... | collective-permute-start | bytes 4616 | tf_op jit(solution)/shard_map/ppermute | solution.py:21
  18.2 136.3 %all-gather.14.cloned.1.call-start = ((), (), s32[]{:S(2)}) async-start(), calls=%async_computation.4 | async-start | bytes 1769472 | tf_op jit(solution)/shard_map/all_gather | solution.py:123
  18.4 19.8 %copy-start.4 = (f32[384]{0:T(512)S(1)}, f32[384]{0:T(512)}, u32[]{:S(2)}) copy-start(f32[384]{0:T(512)} %param.18) | copy-start | bytes 4612
  38.2 23.3 %copy-start.6 = (f32[384]{0:T(512)S(1)}, f32[384]{0:T(512)}, u32[]{:S(2)}) copy-start(f32[384]{0:T(512)} %param.17) | copy-start | bytes 4612
  39.2 4.8 %collective-permute-start.2 = (bf16[384,32]{0,1:T(8,128)(2,1)S(1)}, bf16[384,32]{0,1:T(8,128)(2,1)S(1)}, u32[]{:S(2)}, u32[]{:S(2)}) collective-permute-start(bf16[384,32]{0,1:T(8,128)(2,1)S(1)} %get-tuple-element.6), channel_id=1, source_target_pairs={{0,1},{1,2},{2,3},{3,4},{4,5},{5,6},{6,7},{8,9},{9,10},{10,11},{11... | collective-permute-start | bytes 73736 | tf_op jit(solution)/shard_map/ppermute | solution.py:18
  42.1 5.9 %collective-permute-start.3 = (bf16[384,32]{0,1:T(8,128)(2,1)S(1)}, bf16[384,32]{0,1:T(8,128)(2,1)S(1)}, u32[]{:S(2)}, u32[]{:S(2)}) collective-permute-start(bf16[384,32]{0,1:T(8,128)(2,1)S(1)} %get-tuple-element.5), channel_id=1, source_target_pairs={{1,0},{2,1},{3,2},{4,3},{5,4},{6,5},{7,6},{9,8},{10,9},{11,10},{12... | collective-permute-start | bytes 73736 | tf_op jit(solution)/shard_map/ppermute | solution.py:21
  64.8 32.8 %copy-start.2 = (f32[1536]{0:T(1024)S(1)}, f32[1536]{0:T(1024)}, u32[]{:S(2)}) copy-start(f32[1536]{0:T(1024)} %param.20) | copy-start | bytes 18436
  97.7 31.7 %copy-start.1 = (bf16[1536,256]{1,0:T(8,128)(2,1)S(1)}, bf16[1536,256]{1,0:T(8,128)(2,1)}, u32[]{:S(2)}) copy-start(bf16[1536,256]{1,0:T(8,128)(2,1)} %param.22) | copy-start | bytes 2359300
Sparse Core Ops, SparseCore 0:
  8.9 27.0 all-gather.5
  37.6 23.8 all-gather.7
  63.1 30.7 all-gather.9
  95.4 30.6 all-gather.11
  129.1 25.4 all-gather.13
where the time goes:
time: 167 us
  waiting for transfers between devices  99.6 us (60%)
  blocking collectives  16.5 us (10%)
  matrix products  14.7 us (9%)
  between operations  13.4 us (8%)
  starting transfers between devices  11.5 us (7%)
  other arithmetic  5.76 us (3%)
  local copies, waits for them, and re-layouts  5.2 us (3%)
    all_gather x1, waiting for transfers between devices, shards(): lax.all_gather(pool_weight, 'seq', axis=2, tiled=True)  29.1 us
    all_gather x1, waiting for transfers between devices, shards(): lax.all_gather(value_weight, 'seq', axis=0, tiled=True)  28.4 us
    all_gather x1, blocking collectives, shards(): lax.all_gather(keys, 'seq', axis=0, tiled=True)  16.5 us
    all_gather x1, waiting for transfers between devices, shards(): lax.all_gather(near_weight, 'seq', axis=1, tiled=True)  14.7 us
    all_gather x1, waiting for transfers between devices, shards(): lax.all_gather(dilated_weight, 'seq', axis=1, tiled=True)  13.4 us
    ppermute x2, starting transfers between devices, padded_2(): lax.ppermute(lax.slice_in_dim(block, block.shape[dim] - width, None, axis...  7.47 us
    all_gather x1, waiting for transfers between devices, shards(): lax.all_gather(values, 'seq', axis=0, tiled=True)  7.12 us
    dot_general x2, matrix products, convolution_taps(): jnp.einsum('toc,tcl->ol', weight, stacked, preferred_element_type=jnp.flo...  5.05 us
  transfers between devices with their start and end apart: 9, of which 7 were waited for; matrix products, arithmetic and copies ran while one was open for 10% of the time, Pallas kernels for 0%

commit v1 on v0

--- a/solution.py
+++ b/solution.py
@@ -1,6 +1,10 @@
+import functools
+
 import jax
 import jax.numpy as jnp
 from jax import lax
+from jax.experimental import pallas as pl
+from jax.experimental.pallas import tpu as pltpu
 from jax.sharding import PartitionSpec as P
 
 HEADS = 4
@@ -129,6 +133,426 @@
     denom = jnp.repeat(jnp.transpose(final_sum), VAL, axis=1)
     return (final_acc / denom).astype(jnp.bfloat16)
 
+def fused_body(
+    nz,
+    x_ref,
+    near_ref,
+    dil_ref,
+    pool_ref,
+    val_ref,
+    chan_ref,
+    gain_ref,
+    qw_ref,
+    kw_ref,
+    out_ref,
+    x_s,
+    g_near,
+    g_dil,
+    g_pool,
+    g_val,
+    g_k,
+    g_v,
+    taps_s,
+    pooled_s,
+    ssem,
+    rsem,
+    lsem,
+):
+    n = 2 * nz
+    w = lax.axis_index("win")
+    s0 = lax.axis_index("seq")
+    z = s0 // 2
+    c = s0 % 2
+    wx = w + 1 - 2 * (w % 2)
+    wy = w + 2 - 4 * (w // 2)
+    wg = wy + 1 - 2 * (w % 2)
+    partner = s0 + 1 - 2 * c
+    cross = s0 - 1 + 2 * c
+    cross_ok = jnp.logical_and(cross >= 0, cross < n)
+    local = x_ref.shape[1]
+    ups = {"u": z + 1 < nz, "d": z > 0}
+    steps = [(way, d) for d in range(1, nz) for way in ("u", "d")]
+
+    def exists(way, d):
+        return z >= d if way == "u" else z + d < nz
+
+    def shard_of(way, d, core):
+        return 2 * (z - d if way == "u" else z + d) + core
+
+    def onward(way):
+        return {"win": w, "seq": s0 + 2 if way == "u" else s0 - 2}
+
+    to_x = {"win": wx, "seq": s0}
+    to_y = {"win": wy, "seq": s0}
+    to_c = {"win": w, "seq": partner}
+
+    table = {}
+    pending = []
+
+    def remote(label, src, dst, device):
+        index = table.setdefault(label, len(table))
+        return pltpu.make_async_remote_copy(
+            src_ref=src,
+            dst_ref=dst,
+            send_sem=ssem.at[index],
+            recv_sem=rsem.at[index],
+            device_id=device,
+            device_id_type=pl.DeviceIdType.MESH,
+        )
+
+    def send(cond, label, src, dst, device):
+        def go():
+            remote(label, src(), dst(), device).start()
+
+        def end():
+            remote(label, src(), dst(), device).wait_send()
+
+        if cond is None:
+            go()
+        else:
+            pl.when(cond)(go)
+        pending.append((cond, end))
+
+    def receive(label, dst):
+        remote(label, dst, dst, to_c).wait_recv()
+
+    sources = {"A": near_ref, "B": dil_ref, "C": pool_ref, "D": val_ref}
+    held = {"A": g_near, "B": g_dil, "C": g_pool, "D": g_val, "K": g_k, "V": g_v}
+    by_x = {"A": True, "B": False, "C": True, "D": False}
+
+    def part(ref, q):
+        rows = ref.shape[0] // 4
+        return ref.at[pl.ds(pl.multiple_of(q * rows, 16), rows)]
+
+    def region(p, s, q):
+        rows = held[p].shape[1] // 4
+        return held[p].at[s, pl.ds(pl.multiple_of(q * rows, 16), rows)]
+
+    def local_copy(p):
+        return pltpu.make_async_copy(sources[p], held[p].at[s0], lsem.at["ABCD".index(p)])
+
+    def begin(p):
+        for way in ("u", "d"):
+            send(
+                ups[way],
+                (p, "z", way, 1),
+                lambda: part(sources[p], w),
+                lambda: region(p, s0, w),
+                onward(way),
+            )
+
+    def begin_core(p):
+        local_copy(p).start()
+        send(None, (p, "c"), lambda: sources[p], lambda: held[p].at[s0], to_c)
+
+    def step1(p):
+        for way, d in steps:
+            s = shard_of(way, d, c)
+            piece = lambda s=s: region(p, s, w)
+            ok = exists(way, d)
+            pl.when(ok)(lambda: receive((p, "z", way, d), piece()))
+            if d + 1 < nz:
+                more = jnp.logical_and(ok, ups[way])
+                send(more, (p, "z", way, d + 1), piece, piece, onward(way))
+            send(ok, (p, "x", way, d), piece, piece, to_x)
+            send(ok, (p, "y", way, d), piece, piece, to_y)
+
+    def step2(p):
+        for way, d in steps:
+            s = shard_of(way, d, c)
+            ok = exists(way, d)
+
+            @pl.when(ok)
+            def _():
+                receive((p, "x", way, d), region(p, s, wx))
+                receive((p, "y", way, d), region(p, s, wy))
+
+            q, device = (wy, to_x) if by_x[p] else (wx, to_y)
+            piece = lambda s=s, q=q: region(p, s, q)
+            send(ok, (p, "g", way, d), piece, piece, device)
+
+    def step3(p):
+        for way, d in steps:
+            s = shard_of(way, d, c)
+            ok = exists(way, d)
+            pl.when(ok)(lambda: receive((p, "g", way, d), region(p, s, wg)))
+            whole = lambda s=s: held[p].at[s]
+            send(ok, (p, "c", way, d), whole, whole, to_c)
+
+    def step4(p):
+        if p in sources:
+            local_copy(p).wait()
+        receive((p, "c"), held[p].at[partner])
+        for way, d in steps:
+            s = shard_of(way, d, 1 - c)
+            pl.when(exists(way, d))(lambda: receive((p, "c", way, d), held[p].at[s]))
+
+    def begin_line(p):
+        mine = lambda: held[p].at[s0]
+        for way in ("u", "d"):
+            send(ups[way], (p, "z", way, 1), mine, mine, onward(way))
+        send(None, (p, "c"), mine, mine, to_c)
+
+    def line(p):
+        for way, d in steps:
+            s = shard_of(way, d, c)
+            whole = lambda s=s: held[p].at[s]
+            ok = exists(way, d)
+            pl.when(ok)(lambda: receive((p, "z", way, d), whole()))
+            if d + 1 < nz:
+                more = jnp.logical_and(ok, ups[way])
+                send(more, (p, "z", way, d + 1), whole, whole, onward(way))
+            send(ok, (p, "c", way, d), whole, whole, to_c)
+
+    barrier = pltpu.get_barrier_semaphore()
+
+    def greet(device):
+        pl.semaphore_signal(
+            barrier, inc=1, device_id=device, device_id_type=pl.DeviceIdType.MESH
+        )
+
+    for device in (to_x, to_y, to_c):
+        greet(device)
+    for cond, device in (
+        (ups["u"], onward("u")),
+        (ups["d"], onward("d")),
+        (cross_ok, {"win": w, "seq": cross}),
+    ):
+        pl.when(cond)(lambda: greet(device))
+    above, below = 1 - (z + 1) // nz, 1 - (nz - z) // nz
+    pl.semaphore_wait(barrier, 3 + above + below + c * above + (1 - c) * below)
+
+    begin("A")
+    right_ok, left_ok = s0 + 1 < n, s0 > 0
+    send(
+        right_ok,
+        "to right",
+        lambda: x_ref.at[:, pl.ds(local - 128, 128)],
+        lambda: x_s.at[:, pl.ds(0, 128)],
+        {"win": w, "seq": s0 + 1},
+    )
+    send(
+        left_ok,
+        "to left",
+        lambda: x_ref.at[:, pl.ds(0, 128)],
+        lambda: x_s.at[:, pl.ds(128 + local, 128)],
+        {"win": w, "seq": s0 - 1},
+    )
+    own_x = pltpu.make_async_copy(x_ref, x_s.at[:, pl.ds(128, local)], lsem.at[4])
+    own_x.start()
+    begin_core("A")
+    for p in "BCD":
+        begin(p)
+        begin_core(p)
+    own_x.wait()
+    pl.when(left_ok)(lambda: receive("to right", x_s.at[:, pl.ds(0, 128)]))
+    pl.when(right_ok)(lambda: receive("to left", x_s.at[:, pl.ds(128 + local, 128)]))
+
+    wide = local + 128
+    place = s0 * local - 64 + lax.broadcasted_iota(jnp.int32, (1, wide), 1)
+    inside = jnp.logical_and(place >= 0, place < n * local)
+
+    def act(field, gain):
+        square = jnp.mean(field * field, axis=0, keepdims=True)
+        scaled = field * lax.rsqrt(square + 1e-06) * gain
+        return gelu(scaled)
+
+    def conv(stack, length, weights):
+        total = None
+        for t in range(KS):
+            taps = weights[:, pl.ds(t * rows, rows), :].reshape(channels, channels)
+            term = jnp.dot(
+                taps, stack[t, :, pl.ds(0, length)], preferred_element_type=jnp.float32
+            )
+            total = term if total is None else total + term
+        return total
+
+    channels = x_ref.shape[0]
+    rows = channels // n
+    x = pltpu.roll(x_s[...].astype(jnp.float32), wide + 64, 1)[:, :wide]
+    x = jnp.where(inside, x, 0.0)
+    near_act = act(x, chan_ref[:, 1:2])
+    for t in range(KS):
+        shift = (2 - t) % wide
+        rolled = near_act if shift == 0 else pltpu.roll(near_act, shift, 1)
+        taps_s[t] = rolled.astype(jnp.bfloat16)
+    step1("A")
+    step2("A")
+    step3("A")
+    step1("B")
+    step4("A")
+    near_out = (x + chan_ref[:, 0:1] + conv(taps_s, wide, g_near)).astype(jnp.bfloat16)
+    step2("B")
+    near_wide = near_out.astype(jnp.float32)
+    far_act = jnp.where(inside, act(near_wide, chan_ref[:, 3:4]), 0.0)
+    step3("B")
+    step1("C")
+    for t in range(KS):
+        rolled = pltpu.roll(far_act, wide - 64 - DILATION_STEP * (t - 2), 1)
+        taps_s[t, :, pl.ds(0, local)] = rolled[:, :local].astype(jnp.bfloat16)
+    own_out = pltpu.roll(near_wide, wide - 64, 1)[:, :local]
+    step2("C")
+    step4("B")
+    far_out = (own_out + chan_ref[:, 2:3] + conv(taps_s, local, g_dil)).astype(jnp.bfloat16)
+    step3("C")
+    step1("D")
+    pool_act = gelu(far_out.astype(jnp.float32)).astype(jnp.bfloat16)
+    half = local // 2
+    row = lax.broadcasted_iota(jnp.int32, (local, local), 0)
+    col = lax.broadcasted_iota(jnp.int32, (local, local), 1)
+    picker = jnp.where(row < half, 2 * row, 2 * (row - half) + 1) == col
+    picked = lax.dot_general(
+        picker.astype(jnp.bfloat16),
+        pool_act,
+        (((1,), (1,)), ((), ())),
+        preferred_element_type=jnp.float32,
+    ).astype(jnp.bfloat16)
+    even, odd = picked[:half], picked[half:]
+    step2("D")
+    step4("C")
+    square = None
+    for j in range(n):
+        chunk = jnp.dot(
+            even, g_pool[j, pl.ds(0, channels), :], preferred_element_type=jnp.float32
+        ) + jnp.dot(
+            odd, g_pool[j, pl.ds(channels, channels), :], preferred_element_type=jnp.float32
+        )
+        pooled_s[j] = chunk
+        term = jnp.sum(chunk * chunk, axis=1, keepdims=True)
+        square = term if square is None else square + term
+    step3("D")
+    depth = pooled_s.shape[2]
+    scale = lax.rsqrt(square / (n * depth) + 1e-06)
+    normed = [
+        (pooled_s[j] * scale * gain_ref[j]).astype(jnp.bfloat16) for j in range(n)
+    ]
+
+    def project(weight):
+        total = None
+        for j in range(n):
+            term = jnp.dot(normed[j], weight(j), preferred_element_type=jnp.float32)
+            total = term if total is None else total + term
+        return total
+
+    keys = project(lambda j: kw_ref[pl.ds(j * depth, depth), :])
+    g_k[s0] = keys.astype(jnp.bfloat16)
+    begin_line("K")
+    step4("D")
+    values = project(lambda j: g_val[j])
+    g_v[s0] = values.astype(jnp.bfloat16)
+    begin_line("V")
+    line("K")
+    queries = project(lambda j: qw_ref[pl.ds(j * depth, depth), :]) * KEY ** (-0.5)
+    queries = queries.astype(jnp.bfloat16)
+    step4("K")
+    lane = lax.broadcasted_iota(jnp.int32, (half, 2 * KEY), 1)
+    weights, sums = [], []
+    for pair in range(HEADS // 2):
+        side = queries[:, pair * 2 * KEY : (pair + 1) * 2 * KEY]
+        both = jnp.concatenate(
+            [jnp.where(lane < KEY, side, 0.0), jnp.where(lane < KEY, 0.0, side)], axis=0
+        ).astype(jnp.bfloat16)
+        scores = lax.dot_general(
+            both,
+            g_k[:, :, pl.ds(pair * 2 * KEY, 2 * KEY)].reshape(n * half, 2 * KEY),
+            (((1,), (1,)), ((), ())),
+            preferred_element_type=jnp.float32,
+        )
+        raised = jnp.exp(scores - jnp.max(scores, axis=1, keepdims=True))
+        sums.append(jnp.sum(raised, axis=1, keepdims=True))
+        weights.append(raised.astype(jnp.bfloat16))
+        if pair == 0:
+            line("V")
+    step4("V")
+    lane = lax.broadcasted_iota(jnp.int32, (half, 2 * VAL), 1)
+    for pair in range(HEADS // 2):
+        span = pl.ds(pair * 2 * VAL, 2 * VAL)
+        summed = jnp.dot(
+            weights[pair],
+            g_v[:, :, span].reshape(n * half, 2 * VAL),
+            preferred_element_type=jnp.float32,
+        )
+        result = summed / sums[pair]
+        out_ref[:, span] = jnp.where(lane < VAL, result[:half], result[half:]).astype(
+            jnp.bfloat16
+        )
+    for cond, end in pending:
+        if cond is None:
+            end()
+        else:
+            pl.when(cond)(end)
+
+
+def gelu(x):
+    return 0.5 * x * (1.0 + lax.erf(x * 0.7071067811865476))
+
+
+def fused(
+    conv_input,
+    near_weight,
+    near_bias,
+    near_gain,
+    dilated_weight,
+    dilated_bias,
+    far_gain,
+    pool_weight,
+    attn_gain,
+    query_weight,
+    key_weight,
+    value_weight,
+):
+    n = lax.axis_size("seq")
+    nz = n // 2
+    channels, local = conv_input.shape
+    half = local // 2
+
+    def flat(weight):
+        rows = weight.shape[0] * weight.shape[1]
+        weight = weight.reshape(rows, channels)
+        return jnp.pad(weight, ((0, -rows % 64), (0, 0)))
+
+    near, dilated = flat(near_weight), flat(dilated_weight)
+    depth = pool_weight.shape[2]
+    pool = pool_weight.reshape(2 * channels, depth)
+    chan = jnp.stack([near_bias, near_gain, dilated_bias, far_gain], axis=1)
+    gain = attn_gain.reshape(n, 1, depth)
+    any_spec = pl.BlockSpec(memory_space=pl.ANY)
+    vmem = pl.BlockSpec(memory_space=pltpu.VMEM)
+    count = (4 * 5 + 2 * 2) * 2 * (nz - 1) + 6 + 2
+    gathered = lambda a: pltpu.VMEM((n,) + a.shape, jnp.bfloat16)
+    wide = local + 128
+    return pl.pallas_call(
+        functools.partial(fused_body, nz),
+        out_shape=jax.ShapeDtypeStruct((half, HEADS * VAL), jnp.bfloat16),
+        in_specs=[any_spec] * 5 + [vmem] * 4,
+        out_specs=vmem,
+        scratch_shapes=[
+            pltpu.VMEM((channels, local + 256), jnp.bfloat16),
+            gathered(near),
+            gathered(dilated),
+            gathered(pool),
+            gathered(value_weight),
+            pltpu.VMEM((n, half, HEADS * KEY), jnp.bfloat16),
+            pltpu.VMEM((n, half, HEADS * VAL), jnp.bfloat16),
+            pltpu.VMEM((KS, channels, wide), jnp.bfloat16),
+            pltpu.VMEM((n, half, depth), jnp.float32),
+            pltpu.SemaphoreType.DMA((count,)),
+            pltpu.SemaphoreType.DMA((count,)),
+            pltpu.SemaphoreType.DMA((5,)),
+        ],
+        compiler_params=pltpu.CompilerParams(collective_id=0, has_side_effects=True),
+    )(
+        conv_input,
+        near,
+        dilated,
+        pool,
+        value_weight,
+        chan,
+        gain,
+        query_weight,
+        key_weight,
+    )
+
 
 def solution(mesh):
     placed = (
@@ -145,6 +569,19 @@
         P(),
         P("seq", None),
     )
+
+    def body(*args):
+        near_weight, value_weight = args[1], args[11]
+        count = lax.axis_size("seq")
+        fits = (
+            lax.axis_size("win") == 4
+            and count % 2 == 0
+            and near_weight.shape[1] % 16 == 0
+            and value_weight.shape[0] % 64 == 0
+            and args[0].shape[1] % 128 == 0
+        )
+        return fused(*args) if fits else shards(*args)
+
     return jax.shard_map(
-        shards, mesh=mesh, in_specs=placed, out_specs=P(("win", "seq"), None), check_vma=False
-    )
+        body, mesh=mesh, in_specs=placed, out_specs=P(("win", "seq"), None), check_vma=False
+    )

time: 167 us -> 95.3 us (0.57)
  waiting for transfers between devices: 99.6 us -> 0 us
  Pallas kernels: 0 us -> 86.1 us
  blocking collectives: 16.5 us -> 0 us
  matrix products: 14.7 us -> 0 us
  between operations: 13.4 us -> 0.02 us
  starting transfers between devices: 11.5 us -> 0 us
  other arithmetic: 5.76 us -> 0.01 us
  local copies, waits for them, and re-layouts: 5.2 us -> 8.87 us
    all_gather x5 -> x0, waiting for transfers between devices: 92.8 us -> none  [the longest x1 29.1 us: shards(): lax.all_gather(pool_weight, 'seq', axis=2, tiled=True)]
    pallas_call x0 -> x1, Pallas kernels: none -> 86.1 us  [fused(): pl.pallas_call(functools.partial(fused_body, nz), out_shape=jax.ShapeDtyp...]
    all_gather x1 -> x0, blocking collectives: 16.5 us -> none  [shards(): lax.all_gather(keys, 'seq', axis=0, tiled=True)]
    dot_general x9 -> x0, matrix products: 14.7 us -> none  [the longest x2 5.05 us: convolution_taps(): jnp.einsum('toc,tcl->ol', weight, stacked, preferred_element_type=jnp.flo...]
    ppermute x4 -> x0, starting transfers between devices: 11.3 us -> none  [the longest x2 7.47 us: padded_2(): lax.ppermute(lax.slice_in_dim(block, block.shape[dim] - width, None, axis...]
    ppermute x4 -> x0, waiting for transfers between devices: 4.68 us -> none  [the longest x2 4.68 us: padded_2(): lax.ppermute(lax.slice_in_dim(block, 0, width, axis=dim), axis, backward)]
    another operation x0 -> x5, local copies, waits for them, and re-layouts: none -> 2.87 us  [fused(): chan = jnp.stack([near_bias, near_gain, dilated_bias, far_gain], axis=1)]
    all_gather x2 -> x0, local copies, waits for them, and re-layouts: 2.78 us -> none  [the longest x1 2.58 us: shards(): lax.all_gather(values, 'seq', axis=0, tiled=True)]
  transfers between devices with their start and end apart: 9 -> 0, of which waited for: 7 -> 0; matrix products, arithmetic and copies ran while one was open for 10% -> 0% of each run, Pallas kernels for 0% -> 0%
where the time goes in v1:
time: 95.3 us; the launch traced here: 95 us
  Pallas kernels  86.1 us (90%)
  local copies, waits for them, and re-layouts  8.87 us (9%)
    pallas_call x1, Pallas kernels, fused(): pl.pallas_call(functools.partial(fused_body, nz), out_shape=jax.ShapeDtyp...  86.1 us
    unnamed x10, local copies, waits for them, and re-layouts  3.24 us
    another operation x5, local copies, waits for them, and re-layouts, fused(): chan = jnp.stack([near_bias, near_gain, dilated_bias, far_gain], axis=1)  2.87 us

profile of v1, /device:TPU:1, one launch (start us, length us, event | category | flops | bytes accessed | tf_op | source)
XLA Modules:
  0.0 95.0 jit_solution(1967415829784004754)
XLA Ops:
  0.0 0.0 copy-start.3
  0.0 0.0 copy-start.1
  0.0 0.7 copy-done.3
  0.7 0.7 stack.16
  1.4 0.7 stack.17
  2.1 0.7 stack.18
  2.7 1.4 %reshape.15.gain_ref = f32[8,1,192]{2,1,0:T(1,128)} reshape(f32[1536]{0:T(1024)} %param.20) | data formatting | bytes 12288 | tf_op jit(solution)/shard_map/reshape | solution.py:518
  4.1 0.0 copy-start.2
  4.1 0.8 copy.20.chan_ref
  4.9 0.0 copy-done.1
  4.9 0.0 copy-start
  4.9 0.7 pad.7.near_ref
  5.6 0.0 copy-done.2
  5.6 0.7 pad.8.dil_ref
  6.3 0.0 copy-done
  6.3 0.9 copy.19
  7.3 86.1 %shard_map.118 = bf16[128,768]{1,0:T(8,128)(2,1)} custom-call(bf16[384,256]{1,0:T(8,128)(2,1)} %x_ref.1, bf16[256,384]{1,0:T(8,128)(2,1)} %pad.7.near_ref, bf16[256,384]{1,0:T(8,128)(2,1)} %pad.8.dil_ref, bf16[768,192]{1,0:T(8,128)(2,1)} %bitcast.3, bf16[192,768]{1,0:T(8,128)(2,1)} %val_ref.1, f32[384,4]{1,0:T(8,128)} %copy.20.chan_ref, ...), custom_call_target="tpu_custom_call" | custom-call | tf_op jit(solution)/shard_map/pallas_call | solution.py:524
  93.4 1.6 %copy.22 = bf16[128,768]{1,0:T(8,128)(2,1)} copy(bf16[128,768]{1,0:T(8,128)(2,1)} %shard_map.118) | data formatting | bytes 393216
  (2 shorter events, 0.0 us)
Async XLA Ops:
  0.0 0.7 copy-start.3
  0.0 4.9 %copy-start.1 = (bf16[5,48,384]{2,1,0:T(8,128)(2,1)S(1)}, bf16[5,48,384]{2,1,0:T(8,128)(2,1)}, u32[]{:S(2)}) copy-start(bf16[5,48,384]{2,1,0:T(8,128)(2,1)} %param.13) | copy-start | bytes 552964
  4.1 1.5 %copy-start.2 = (bf16[5,48,384]{2,1,0:T(8,128)(2,1)S(1)}, bf16[5,48,384]{2,1,0:T(8,128)(2,1)}, u32[]{:S(2)}) copy-start(bf16[5,48,384]{2,1,0:T(8,128)(2,1)} %param.16) | copy-start | bytes 552964
  4.9 1.4 %copy-start = (bf16[2,384,192]{1,2,0:T(8,128)(2,1)S(1)}, bf16[2,384,192]{1,2,0:T(8,128)(2,1)}, u32[]{:S(2)}) copy-start(bf16[2,384,192]{1,2,0:T(8,128)(2,1)} %param.19) | copy-start | bytes 884740

commit v2 on v1

--- a/solution.py
+++ b/solution.py
@@ -140,10 +140,13 @@
     dil_ref,
     pool_ref,
     val_ref,
-    chan_ref,
+    nb_ref,
+    ng_ref,
+    db_ref,
+    fg_ref,
     gain_ref,
-    qw_ref,
-    kw_ref,
+    qw_hbm,
+    kw_hbm,
     out_ref,
     x_s,
     g_near,
@@ -153,7 +156,8 @@
     g_k,
     g_v,
     taps_s,
-    pooled_s,
+    qw_ref,
+    kw_ref,
     ssem,
     rsem,
     lsem,
@@ -220,30 +224,28 @@
     held = {"A": g_near, "B": g_dil, "C": g_pool, "D": g_val, "K": g_k, "V": g_v}
     by_x = {"A": True, "B": False, "C": True, "D": False}
 
-    def part(ref, q):
-        rows = ref.shape[0] // 4
-        return ref.at[pl.ds(pl.multiple_of(q * rows, 16), rows)]
+    def solid(p, s):
+        return held[p].at[s, pl.ds(0, sources[p].shape[0])]
 
     def region(p, s, q):
         rows = held[p].shape[1] // 4
         return held[p].at[s, pl.ds(pl.multiple_of(q * rows, 16), rows)]
 
     def local_copy(p):
-        return pltpu.make_async_copy(sources[p], held[p].at[s0], lsem.at["ABCD".index(p)])
+        return pltpu.make_async_copy(sources[p], solid(p, s0), lsem.at["ABCD".index(p)])
 
     def begin(p):
         for way in ("u", "d"):
             send(
                 ups[way],
                 (p, "z", way, 1),
-                lambda: part(sources[p], w),
+                lambda: region(p, s0, w),
                 lambda: region(p, s0, w),
                 onward(way),
             )
 
     def begin_core(p):
-        local_copy(p).start()
-        send(None, (p, "c"), lambda: sources[p], lambda: held[p].at[s0], to_c)
+        send(None, (p, "c"), lambda: sources[p], lambda: solid(p, s0), to_c)
 
     def step1(p):
         for way, d in steps:
@@ -276,16 +278,15 @@
             s = shard_of(way, d, c)
             ok = exists(way, d)
             pl.when(ok)(lambda: receive((p, "g", way, d), region(p, s, wg)))
-            whole = lambda s=s: held[p].at[s]
+            whole = lambda s=s: solid(p, s)
             send(ok, (p, "c", way, d), whole, whole, to_c)
 
     def step4(p):
-        if p in sources:
-            local_copy(p).wait()
-        receive((p, "c"), held[p].at[partner])
+        view = solid if p in sources else lambda p, s: held[p].at[s]
+        receive((p, "c"), view(p, partner))
         for way, d in steps:
             s = shard_of(way, d, 1 - c)
-            pl.when(exists(way, d))(lambda: receive((p, "c", way, d), held[p].at[s]))
+            pl.when(exists(way, d))(lambda: receive((p, "c", way, d), view(p, s)))
 
     def begin_line(p):
         mine = lambda: held[p].at[s0]
@@ -304,6 +305,16 @@
                 send(more, (p, "z", way, d + 1), whole, whole, onward(way))
             send(ok, (p, "c", way, d), whole, whole, to_c)
 
+    own_x = pltpu.make_async_copy(x_ref, x_s.at[:, pl.ds(128, local)], lsem.at[4])
+    own_q = pltpu.make_async_copy(qw_hbm, qw_ref, lsem.at[5])
+    own_k = pltpu.make_async_copy(kw_hbm, kw_ref, lsem.at[6])
+    local_copy("A").start()
+    own_x.start()
+    for p in "BCD":
+        local_copy(p).start()
+    own_k.start()
+    own_q.start()
+
     barrier = pltpu.get_barrier_semaphore()
 
     def greet(device):
@@ -322,6 +333,7 @@
     above, below = 1 - (z + 1) // nz, 1 - (nz - z) // nz
     pl.semaphore_wait(barrier, 3 + above + below + c * above + (1 - c) * below)
 
+    local_copy("A").wait()
     begin("A")
     right_ok, left_ok = s0 + 1 < n, s0 > 0
     send(
@@ -338,10 +350,9 @@
         lambda: x_s.at[:, pl.ds(128 + local, 128)],
         {"win": w, "seq": s0 - 1},
     )
-    own_x = pltpu.make_async_copy(x_ref, x_s.at[:, pl.ds(128, local)], lsem.at[4])
-    own_x.start()
     begin_core("A")
     for p in "BCD":
+        local_copy(p).wait()
         begin(p)
         begin_core(p)
     own_x.wait()
@@ -369,33 +380,41 @@
 
     channels = x_ref.shape[0]
     rows = channels // n
+    diagonal = lax.broadcasted_iota(
+        jnp.int32, (channels, channels), 0
+    ) == lax.broadcasted_iota(jnp.int32, (channels, channels), 1)
+
+    def column(ref):
+        return jnp.sum(jnp.where(diagonal, ref[...].reshape(1, channels), 0.0), axis=1, keepdims=True)
+
     x = pltpu.roll(x_s[...].astype(jnp.float32), wide + 64, 1)[:, :wide]
     x = jnp.where(inside, x, 0.0)
-    near_act = act(x, chan_ref[:, 1:2])
+    near_act = act(x, column(ng_ref))
     for t in range(KS):
         shift = (2 - t) % wide
         rolled = near_act if shift == 0 else pltpu.roll(near_act, shift, 1)
         taps_s[t] = rolled.astype(jnp.bfloat16)
     step1("A")
     step2("A")
+    step1("B")
     step3("A")
-    step1("B")
+    step2("B")
+    step1("C")
     step4("A")
-    near_out = (x + chan_ref[:, 0:1] + conv(taps_s, wide, g_near)).astype(jnp.bfloat16)
-    step2("B")
+    near_out = (x + column(nb_ref) + conv(taps_s, wide, g_near)).astype(jnp.bfloat16)
+    step3("B")
+    step2("C")
     near_wide = near_out.astype(jnp.float32)
-    far_act = jnp.where(inside, act(near_wide, chan_ref[:, 3:4]), 0.0)
-    step3("B")
-    step1("C")
+    far_act = jnp.where(inside, act(near_wide, column(fg_ref)), 0.0)
+    step1("D")
     for t in range(KS):
         rolled = pltpu.roll(far_act, wide - 64 - DILATION_STEP * (t - 2), 1)
         taps_s[t, :, pl.ds(0, local)] = rolled[:, :local].astype(jnp.bfloat16)
     own_out = pltpu.roll(near_wide, wide - 64, 1)[:, :local]
-    step2("C")
     step4("B")
-    far_out = (own_out + chan_ref[:, 2:3] + conv(taps_s, local, g_dil)).astype(jnp.bfloat16)
     step3("C")
-    step1("D")
+    far_out = (own_out + column(db_ref) + conv(taps_s, local, g_dil)).astype(jnp.bfloat16)
+    step2("D")
     pool_act = gelu(far_out.astype(jnp.float32)).astype(jnp.bfloat16)
     half = local // 2
     row = lax.broadcasted_iota(jnp.int32, (local, local), 0)
@@ -408,41 +427,36 @@
         preferred_element_type=jnp.float32,
     ).astype(jnp.bfloat16)
     even, odd = picked[:half], picked[half:]
-    step2("D")
     step4("C")
-    square = None
-    for j in range(n):
-        chunk = jnp.dot(
-            even, g_pool[j, pl.ds(0, channels), :], preferred_element_type=jnp.float32
-        ) + jnp.dot(
-            odd, g_pool[j, pl.ds(channels, channels), :], preferred_element_type=jnp.float32
-        )
-        pooled_s[j] = chunk
-        term = jnp.sum(chunk * chunk, axis=1, keepdims=True)
-        square = term if square is None else square + term
+    depth = pool_ref.shape[0] // 2
+    features = n * depth
+
+    def pool(rows_of, tap):
+        taps = g_pool[:, pl.ds(tap * depth, depth), :].reshape(features, channels)
+        return lax.dot_general(
+            rows_of, taps, (((1,), (1,)), ((), ())), preferred_element_type=jnp.float32
+        )
+
+    pooled = pool(even, 0) + pool(odd, 1)
+    square = jnp.mean(pooled * pooled, axis=1, keepdims=True)
+    gain = gain_ref[...].reshape(1, features)
+    normed = (pooled * lax.rsqrt(square + 1e-06) * gain).astype(jnp.bfloat16)
     step3("D")
-    depth = pooled_s.shape[2]
-    scale = lax.rsqrt(square / (n * depth) + 1e-06)
-    normed = [
-        (pooled_s[j] * scale * gain_ref[j]).astype(jnp.bfloat16) for j in range(n)
-    ]
+    own_k.wait()
+    own_q.wait()
 
     def project(weight):
-        total = None
-        for j in range(n):
-            term = jnp.dot(normed[j], weight(j), preferred_element_type=jnp.float32)
-            total = term if total is None else total + term
-        return total
-
-    keys = project(lambda j: kw_ref[pl.ds(j * depth, depth), :])
+        return jnp.dot(normed, weight, preferred_element_type=jnp.float32)
+
+    keys = project(kw_ref[...])
     g_k[s0] = keys.astype(jnp.bfloat16)
     begin_line("K")
     step4("D")
-    values = project(lambda j: g_val[j])
+    values = project(g_val[...].reshape(features, HEADS * VAL))
     g_v[s0] = values.astype(jnp.bfloat16)
     begin_line("V")
     line("K")
-    queries = project(lambda j: qw_ref[pl.ds(j * depth, depth), :]) * KEY ** (-0.5)
+    queries = project(qw_ref[...]) * KEY ** (-0.5)
     queries = queries.astype(jnp.bfloat16)
     step4("K")
     lane = lax.broadcasted_iota(jnp.int32, (half, 2 * KEY), 1)
@@ -507,24 +521,19 @@
     half = local // 2
 
     def flat(weight):
-        rows = weight.shape[0] * weight.shape[1]
-        weight = weight.reshape(rows, channels)
-        return jnp.pad(weight, ((0, -rows % 64), (0, 0)))
+        return weight.reshape(weight.shape[0] * weight.shape[1], channels)
 
     near, dilated = flat(near_weight), flat(dilated_weight)
-    depth = pool_weight.shape[2]
-    pool = pool_weight.reshape(2 * channels, depth)
-    chan = jnp.stack([near_bias, near_gain, dilated_bias, far_gain], axis=1)
-    gain = attn_gain.reshape(n, 1, depth)
+    pool = flat(jnp.transpose(pool_weight, (0, 2, 1)))
     any_spec = pl.BlockSpec(memory_space=pl.ANY)
     vmem = pl.BlockSpec(memory_space=pltpu.VMEM)
     count = (4 * 5 + 2 * 2) * 2 * (nz - 1) + 6 + 2
-    gathered = lambda a: pltpu.VMEM((n,) + a.shape, jnp.bfloat16)
+    gathered = lambda a: pltpu.VMEM((n, a.shape[0] + -a.shape[0] % 64, a.shape[1]), jnp.bfloat16)
     wide = local + 128
     return pl.pallas_call(
         functools.partial(fused_body, nz),
         out_shape=jax.ShapeDtypeStruct((half, HEADS * VAL), jnp.bfloat16),
-        in_specs=[any_spec] * 5 + [vmem] * 4,
+        in_specs=[any_spec] * 5 + [vmem] * 5 + [any_spec] * 2,
         out_specs=vmem,
         scratch_shapes=[
             pltpu.VMEM((channels, local + 256), jnp.bfloat16),
@@ -535,10 +544,11 @@
             pltpu.VMEM((n, half, HEADS * KEY), jnp.bfloat16),
             pltpu.VMEM((n, half, HEADS * VAL), jnp.bfloat16),
             pltpu.VMEM((KS, channels, wide), jnp.bfloat16),
-            pltpu.VMEM((n, half, depth), jnp.float32),
+            pltpu.VMEM(query_weight.shape, jnp.bfloat16),
+            pltpu.VMEM(key_weight.shape, jnp.bfloat16),
             pltpu.SemaphoreType.DMA((count,)),
             pltpu.SemaphoreType.DMA((count,)),
-            pltpu.SemaphoreType.DMA((5,)),
+            pltpu.SemaphoreType.DMA((7,)),
         ],
         compiler_params=pltpu.CompilerParams(collective_id=0, has_side_effects=True),
     )(
@@ -547,8 +557,11 @@
         dilated,
         pool,
         value_weight,
-        chan,
-        gain,
+        near_bias,
+        near_gain,
+        dilated_bias,
+        far_gain,
+        attn_gain,
         query_weight,
         key_weight,
     )

time: 95.3 us -> 74.6 us (0.78)
  Pallas kernels: 86.1 us -> 72.8 us
  local copies, waits for them, and re-layouts: 8.87 us -> 1.62 us
    pallas_call x1, Pallas kernels: 86.1 us -> 72.8 us  [fused(): pl.pallas_call(functools.partial(fused_body, nz), out_shape=jax.ShapeDtyp...]
    another operation x5 -> x0, local copies, waits for them, and re-layouts: 2.87 us -> none  [fused(): chan = jnp.stack([near_bias, near_gain, dilated_bias, far_gain], axis=1)]
    unnamed x10 -> x1, local copies, waits for them, and re-layouts: 3.24 us -> 1.62 us
    pad x2 -> x0, local copies, waits for them, and re-layouts: 1.39 us -> none  [flat(): return jnp.pad(weight, ((0, -rows % 64), (0, 0)))]
    reshape x1 -> x0, local copies, waits for them, and re-layouts: 1.37 us -> none  [fused(): gain = attn_gain.reshape(n, 1, depth)]
where the time goes in v2:
time: 74.6 us; the launch traced here: 74.5 us
  Pallas kernels  72.8 us (98%)
  local copies, waits for them, and re-layouts  1.62 us (2%)
    pallas_call x1, Pallas kernels, fused(): pl.pallas_call(functools.partial(fused_body, nz), out_shape=jax.ShapeDtyp...  72.8 us
    unnamed x1, local copies, waits for them, and re-layouts  1.62 us

profile of v2, /device:TPU:1, one launch (start us, length us, event | category | flops | bytes accessed | tf_op | source)
XLA Modules:
  0.0 74.5 jit_solution(11662806347363818152)
XLA Ops:
  0.0 72.8 %shard_map.118 = bf16[128,768]{1,0:T(8,128)(2,1)} custom-call(bf16[384,256]{1,0:T(8,128)(2,1)} %x_ref.1, bf16[240,384]{1,0:T(8,128)(2,1)} %bitcast.6, bf16[240,384]{1,0:T(8,128)(2,1)} %bitcast.7, bf16[384,384]{1,0:T(8,128)(2,1)} %bitcast.5, bf16[192,768]{1,0:T(8,128)(2,1)} %val_ref.1, f32[384]{0:T(512)} %nb_ref.1, f32[384]{0:T(512)} %ng_ref.1, f32[384]{0:T(512)} %db_ref.1, ...), custom_call_target="tpu_custom_call" | custom-call | tf_op jit(solution)/shard_map/pallas_call | solution.py:533
  72.8 1.6 %copy.14 = bf16[128,768]{1,0:T(8,128)(2,1)} copy(bf16[128,768]{1,0:T(8,128)(2,1)} %shard_map.118) | data formatting | bytes 393216

commit v3 on v2

--- a/solution.py
+++ b/solution.py
@@ -441,7 +441,6 @@
     square = jnp.mean(pooled * pooled, axis=1, keepdims=True)
     gain = gain_ref[...].reshape(1, features)
     normed = (pooled * lax.rsqrt(square + 1e-06) * gain).astype(jnp.bfloat16)
-    step3("D")
     own_k.wait()
     own_q.wait()
 
@@ -451,6 +450,7 @@
     keys = project(kw_ref[...])
     g_k[s0] = keys.astype(jnp.bfloat16)
     begin_line("K")
+    step3("D")
     step4("D")
     values = project(g_val[...].reshape(features, HEADS * VAL))
     g_v[s0] = values.astype(jnp.bfloat16)

time: 74.6 us -> 72.7 us (0.975)
  Pallas kernels: 72.8 us -> 70.9 us
    pallas_call x1, Pallas kernels: 72.8 us -> 70.9 us  [fused(): pl.pallas_call(functools.partial(fused_body, nz), out_shape=jax.ShapeDtyp...]
where the time goes in v3:
time: 72.7 us; the launch traced here: 72.5 us
  Pallas kernels  70.9 us (98%)
  local copies, waits for them, and re-layouts  1.62 us (2%)
    pallas_call x1, Pallas kernels, fused(): pl.pallas_call(functools.partial(fused_body, nz), out_shape=jax.ShapeDtyp...  70.9 us
    unnamed x1, local copies, waits for them, and re-layouts  1.62 us

profile of v3, /device:TPU:1, one launch (start us, length us, event | category | flops | bytes accessed | tf_op | source)
XLA Modules:
  0.0 72.5 jit_solution(5308341323910398276)
XLA Ops:
  0.0 70.9 %shard_map.118 = bf16[128,768]{1,0:T(8,128)(2,1)} custom-call(bf16[384,256]{1,0:T(8,128)(2,1)} %x_ref.1, bf16[240,384]{1,0:T(8,128)(2,1)} %bitcast.6, bf16[240,384]{1,0:T(8,128)(2,1)} %bitcast.7, bf16[384,384]{1,0:T(8,128)(2,1)} %bitcast.5, bf16[192,768]{1,0:T(8,128)(2,1)} %val_ref.1, f32[384]{0:T(512)} %nb_ref.1, f32[384]{0:T(512)} %ng_ref.1, f32[384]{0:T(512)} %db_ref.1, ...), custom_call_target="tpu_custom_call" | custom-call | tf_op jit(solution)/shard_map/pallas_call | solution.py:533
  70.9 1.6 %copy.14 = bf16[128,768]{1,0:T(8,128)(2,1)} copy(bf16[128,768]{1,0:T(8,128)(2,1)} %shard_map.118) | data formatting | bytes 393216
